TPU v7x, 32 devices: a whole 2x2x4 slice. The times are simulated.
32 devices in a mesh: dp: 8 (over z, y), tensor: 4 (over x, core).
Axes of the slice: x: 2, y: 2, z: 4, core: 2. Of those that a mesh axis runs over, the one named last changes fastest.
Arguments:
- inputs: bfloat16 [16384, 2048], P(('dp', 'tensor')), may hold values from -6 to 6
- lengths: int32 [8], P('dp'), may hold values from 128 to 2048, as said below
- ln1_gain: bfloat16 [2048], replicated, may hold values from 0.5 to 1.5
- ln1_bias: bfloat16 [2048], replicated, may hold values from -1 to 1
- ln2_gain: bfloat16 [2048], replicated, may hold values from 0.5 to 1.5
- ln2_bias: bfloat16 [2048], replicated, may hold values from -1 to 1
- w_qkv: bfloat16 [2048, 6144], P(None, 'tensor'), may hold values from -0.1875 to 0.1875
- b_qkv: bfloat16 [6144], P('tensor'), may hold values from -1 to 1
- w_dense: bfloat16 [2048, 2048], P('tensor'), may hold values from -0.5 to 0.5
- b_dense: bfloat16 [2048], replicated, may hold values from -1 to 1
- w_fc1: bfloat16 [2048, 8192], P(None, 'tensor'), may hold values from -0.125 to 0.125
- b_fc1: bfloat16 [8192], P('tensor'), may hold values from -1 to 1
- w_fc2: bfloat16 [8192, 2048], P('tensor'), may hold values from -0.09375 to 0.09375
- b_fc2: bfloat16 [2048], replicated, may hold values from -1 to 1
- out_grad: bfloat16 [16384, 2048], P(('dp', 'tensor')), may hold values from -6 to 6
Outputs:
- outputs: bfloat16 [16384, 2048], P(('dp', 'tensor'))
- in_grad: float32 [16384, 2048], P(('dp', 'tensor'))
- g_ln1_gain: float32 [2048], replicated
- g_ln1_bias: float32 [2048], replicated
- g_ln2_gain: float32 [2048], replicated
- g_ln2_bias: float32 [2048], replicated
- g_w_qkv: float32 [2048, 6144], P(None, 'tensor')
- g_b_qkv: float32 [6144], P('tensor')
- g_w_dense: float32 [2048, 2048], P('tensor')
- g_b_dense: float32 [2048], replicated
- g_w_fc1: float32 [2048, 8192], P(None, 'tensor')
- g_b_fc1: float32 [8192], P('tensor')
- g_w_fc2: float32 [8192, 2048], P('tensor')
- g_b_fc2: float32 [2048], replicated
Inputs may be any that keep to these rules, and one draw needn't show every extreme that they name: `lengths`: tokens of a sequence at places from its length on are padding; at least one sequence has length exactly 2048 and one exactly 128.
All inputs are finite; a program needn't handle non-finite values.
Results may differ from a plain program's by a relative error of at most 0.014.
The roundings to bfloat16 on the way count: a program that leaves them out, or rounds other values in their place, can miss the bound.
Values may be sent and summed in bfloat16 or wider, within the bound.
No kernel may reach another device: no remote copies, remote signals or barrier semaphores. Data moves between devices by JAX's collectives and lax.ppermute only.
A program may use at most 320 MiB of HBM per device.

v0:
```python
from functools import partial
import jax
import jax.numpy as jnp
from jax import lax
from jax.sharding import PartitionSpec as P

HD = 128
ROT = 32
SEQ = 2048


def layer_norm(values, gain_vec, offset):
    average = jnp.mean(values, axis=-1, keepdims=True)
    centred = values - average
    spread = jnp.mean(centred * centred, axis=-1, keepdims=True)
    return centred * lax.rsqrt(spread + 1e-05) * gain_vec + offset


def rotary_tables(positions):
    places = jnp.arange(positions, dtype=jnp.float32)
    halves = jnp.arange(ROT // 2, dtype=jnp.float32)
    inverse = 10000.0 ** (-2.0 * halves / ROT)
    angles = places[:, None] * inverse[None, :]
    angles = jnp.concatenate([angles, angles], axis=1)
    return (jnp.cos(angles), jnp.sin(angles))


def rotate(block_data, cos_table, sin_table):
    turned = block_data[..., :ROT]
    front_half = turned[..., : ROT // 2]
    back_half = turned[..., ROT // 2 :]
    swapped = jnp.concatenate([-back_half, front_half], axis=-1)
    result = turned * cos_table[:, None, :] + swapped * sin_table[:, None, :]
    return jnp.concatenate([result, block_data[..., ROT:]], axis=-1)


def contract_rows(left, right):
    return lax.dot_general(
        left, right, (((0,), (0,)), ((), ())), preferred_element_type=jnp.float32
    )


def times_transposed(left, right):
    return lax.dot_general(
        left, right, (((1,), (1,)), ((), ())), preferred_element_type=jnp.float32
    )


def shards(
    inputs,
    lengths,
    ln1_gain,
    ln1_bias,
    ln2_gain,
    ln2_bias,
    w_qkv,
    b_qkv,
    w_dense,
    b_dense,
    w_fc1,
    b_fc1,
    w_fc2,
    b_fc2,
    out_grad,
):
    own_rows = inputs.shape[0]
    width = inputs.shape[1]
    seq_count = lengths.shape[0]
    heads_here = w_dense.shape[0] // HD
    group_rows = own_rows * lax.axis_size("tensor")
    block = min(512, SEQ)
    block_count = SEQ // block
    scale = HD ** (-0.5)
    row_floats = inputs.astype(jnp.float32)
    gain_first = ln1_gain.astype(jnp.float32)
    gain_second = ln2_gain.astype(jnp.float32)
    normed_one, back_one = jax.vjp(layer_norm, row_floats, gain_first, ln1_bias.astype(jnp.float32))
    normed_two, back_two = jax.vjp(
        layer_norm, row_floats, gain_second, ln2_bias.astype(jnp.float32)
    )
    whole_one, whole_two = (
        lax.all_gather(normed_one.astype(jnp.bfloat16), "tensor", axis=0, tiled=True),
        lax.all_gather(normed_two.astype(jnp.bfloat16), "tensor", axis=0, tiled=True),
    )
    packed = jnp.dot(whole_one, w_qkv, preferred_element_type=jnp.float32) + b_qkv.astype(
        jnp.float32
    )
    packed = packed.reshape(seq_count, SEQ, heads_here, 3, HD)
    cos_table, sin_table = rotary_tables(SEQ)

    def prepare(raw_query, raw_keys):
        return (
            rotate(raw_query, cos_table, sin_table) * scale,
            rotate(raw_keys, cos_table, sin_table),
        )

    turned_query, turned_keys = prepare(packed[:, :, :, 0], packed[:, :, :, 1])
    queries = turned_query.astype(jnp.bfloat16).transpose(0, 2, 1, 3)
    key_rows = turned_keys.astype(jnp.bfloat16).transpose(0, 2, 1, 3)
    value_rows = packed[:, :, :, 2].astype(jnp.bfloat16).transpose(0, 2, 1, 3)
    places = jnp.arange(SEQ)
    key_valid = places[None, :] < lengths[:, None]
    validity = key_valid.astype(jnp.float32)

    def block_scores(start):
        query_block = lax.dynamic_slice_in_dim(queries, start, block, 2)
        scores = jnp.einsum(
            "bhqd,bhkd->bhqk", query_block, key_rows, preferred_element_type=jnp.float32
        )
        query_places = start + jnp.arange(block)
        allowed = (places[None, :] <= query_places[:, None])[None, None] & key_valid[
            :, None, None, :
        ]
        return (query_block, jnp.where(allowed, scores, -1e30))

    def forward_block(start):
        _, masked = block_scores(start)
        highest = jnp.max(masked, axis=3, keepdims=True)
        weights = jnp.exp(masked - highest)
        totals = jnp.sum(weights, axis=3, keepdims=True)
        attn_probs = weights / totals
        context_block = jnp.einsum(
            "bhqk,bhkd->bhqd",
            attn_probs.astype(jnp.bfloat16),
            value_rows,
            preferred_element_type=jnp.float32,
        )
        return (context_block, highest, totals)

    starts = jnp.arange(block_count) * block
    context_blocks, highest_all, totals_all = lax.map(forward_block, starts)
    context = (
        context_blocks.transpose(1, 0, 3, 2, 4).reshape(seq_count, SEQ, heads_here, HD)
        * validity[:, :, None, None]
    )
    context = context.astype(jnp.bfloat16).reshape(group_rows, heads_here * HD)
    hidden = jnp.dot(whole_two, w_fc1, preferred_element_type=jnp.float32) + b_fc1.astype(
        jnp.float32
    )
    active = jax.nn.gelu(hidden, approximate=False).astype(jnp.bfloat16)
    branches = lax.psum_scatter(
        jnp.dot(context, w_dense, preferred_element_type=jnp.float32)
        + jnp.dot(active, w_fc2, preferred_element_type=jnp.float32),
        "tensor",
        scatter_dimension=0,
        tiled=True,
    )
    outputs = (
        row_floats + branches + b_dense.astype(jnp.float32) + b_fc2.astype(jnp.float32)
    ).astype(jnp.bfloat16)
    grad_rows = lax.all_gather(out_grad, "tensor", axis=0, tiled=True)
    out_bias_grad = jnp.sum(grad_rows, axis=0, dtype=jnp.float32)
    dense_grad = contract_rows(context, grad_rows)
    fc2_grad = contract_rows(active, grad_rows)
    _, gelu_back = jax.vjp(partial(jax.nn.gelu, approximate=False), hidden)
    hidden_grad = gelu_back(times_transposed(grad_rows, w_fc2))[0].astype(jnp.bfloat16)
    fc1_grad = contract_rows(whole_two, hidden_grad)
    fc1_bias_grad = jnp.sum(hidden_grad, axis=0, dtype=jnp.float32)
    context_grad = (
        times_transposed(grad_rows, w_dense)
        .astype(jnp.bfloat16)
        .reshape(seq_count, SEQ, heads_here, HD)
    )
    context_grad = (context_grad * validity[:, :, None, None].astype(jnp.bfloat16)).transpose(
        0, 2, 1, 3
    )

    def backward_block(carry, element):
        key_grad, value_grad = carry
        start, highest, totals = element
        query_block, masked = block_scores(start)
        attn_probs = jnp.exp(masked - highest) / totals
        grad_block = lax.dynamic_slice_in_dim(context_grad, start, block, 2)
        probs_grad = jnp.einsum(
            "bhqd,bhkd->bhqk", grad_block, value_rows, preferred_element_type=jnp.float32
        )
        centre = jnp.sum(attn_probs * probs_grad, axis=3, keepdims=True)
        score_grad = (attn_probs * (probs_grad - centre)).astype(jnp.bfloat16)
        query_grad = jnp.einsum(
            "bhqk,bhkd->bhqd", score_grad, key_rows, preferred_element_type=jnp.float32
        )
        key_grad = key_grad + jnp.einsum(
            "bhqk,bhqd->bhkd", score_grad, query_block, preferred_element_type=jnp.float32
        )
        value_grad = value_grad + jnp.einsum(
            "bhqk,bhqd->bhkd",
            attn_probs.astype(jnp.bfloat16),
            grad_block,
            preferred_element_type=jnp.float32,
        )
        return ((key_grad, value_grad), query_grad)

    zero_grads = jnp.zeros((seq_count, heads_here, SEQ, HD), jnp.float32)
    (key_grad, value_grad), query_blocks = lax.scan(
        backward_block, (zero_grads, zero_grads), (starts, highest_all, totals_all)
    )
    query_grad = query_blocks.transpose(1, 0, 3, 2, 4).reshape(seq_count, SEQ, heads_here, HD)
    _, prepare_back = jax.vjp(prepare, packed[:, :, :, 0], packed[:, :, :, 1])
    raw_query_grad, raw_key_grad = prepare_back((query_grad, key_grad.transpose(0, 2, 1, 3)))
    packed_grad = jnp.stack(
        [raw_query_grad, raw_key_grad, value_grad.transpose(0, 2, 1, 3)], axis=3
    )
    packed_grad = packed_grad.astype(jnp.bfloat16).reshape(group_rows, 3 * heads_here * HD)
    qkv_grad = contract_rows(whole_one, packed_grad)
    qkv_bias_grad = jnp.sum(packed_grad, axis=0, dtype=jnp.float32)
    normed_grads = lax.psum_scatter(
        jnp.concatenate(
            [times_transposed(packed_grad, w_qkv), times_transposed(hidden_grad, w_fc1)], axis=1
        ).astype(jnp.bfloat16),
        "tensor",
        scatter_dimension=0,
        tiled=True,
    ).astype(jnp.float32)
    input_one, gain_one, bias_one = back_one(normed_grads[:, :width])
    input_two, gain_two, bias_two = back_two(normed_grads[:, width:])
    in_grad = out_grad.astype(jnp.float32) + input_one + input_two
    gain_one, bias_one, gain_two, bias_two = lax.psum(
        (gain_one, bias_one, gain_two, bias_two), ("dp", "tensor")
    )
    qkv_grad, qkv_bias_grad, dense_grad, fc1_grad, fc1_bias_grad, fc2_grad, out_bias_grad = (
        lax.psum(qkv_grad.astype(jnp.bfloat16), "dp").astype(jnp.float32),
        lax.psum(qkv_bias_grad.astype(jnp.bfloat16), "dp").astype(jnp.float32),
        lax.psum(dense_grad.astype(jnp.bfloat16), "dp").astype(jnp.float32),
        lax.psum(fc1_grad.astype(jnp.bfloat16), "dp").astype(jnp.float32),
        lax.psum(fc1_bias_grad.astype(jnp.bfloat16), "dp").astype(jnp.float32),
        lax.psum(fc2_grad.astype(jnp.bfloat16), "dp").astype(jnp.float32),
        lax.psum(out_bias_grad.astype(jnp.bfloat16), "dp").astype(jnp.float32),
    )
    return (
        outputs,
        in_grad,
        gain_one,
        bias_one,
        gain_two,
        bias_two,
        qkv_grad,
        qkv_bias_grad,
        dense_grad,
        out_bias_grad,
        fc1_grad,
        fc1_bias_grad,
        fc2_grad,
        out_bias_grad,
    )


def solution(mesh):
    placed = (
        P(("dp", "tensor"), None),
        P("dp"),
        P(),
        P(),
        P(),
        P(),
        P(None, "tensor"),
        P("tensor"),
        P("tensor", None),
        P(),
        P(None, "tensor"),
        P("tensor"),
        P("tensor", None),
        P(),
        P(("dp", "tensor"), None),
    )
    return jax.shard_map(
        shards,
        mesh=mesh,
        in_specs=placed,
        out_specs=(
            P(("dp", "tensor"), None),
            P(("dp", "tensor"), None),
            P(),
            P(),
            P(),
            P(),
            P(None, "tensor"),
            P("tensor"),
            P("tensor", None),
            P(),
            P(None, "tensor"),
            P("tensor"),
            P("tensor", None),
            P(),
        ),
        check_vma=False,
    )
```

profile of v0, /device:TPU:0, one launch (start us, length us, event | category | flops | bytes accessed | tf_op | source)
XLA Modules:
  0.0 1759.9 jit_solution(367036084671340730)
XLA Ops:
  24.9 52.2 %all-gather.4.cloned.1.call-done = bf16[2048,2048]{1,0:T(8,128)(2,1)} async-done(((bf16[512,2048]{1,0:T(8,128)(2,1)}), bf16[2048,2048]{1,0:T(8,128)(2,1)}) %all-gather.4.cloned.1.call-update) | async-done | bytes 8388624 | tf_op jit(solution)/shard_map/all_gather | solution.py:82
  77.0 18.0 %convolution_add_fusion = f32[2048,1536]{0,1:T(8,128)S(1)} fusion(bf16[2048,2048]{1,0:T(8,128)(2,1)} %all-gather.4.cloned.1.call-done, bf16[2048,1536]{1,0:T(8,128)(2,1)} %param.25, f32[1536]{0:T(1024)S(1)} %convert_element_type.182), kind=kOutput, calls=%fused_computation.75 | convolution fusion | flops 12888047616 | bytes 27269120 | tf_op jit(solution)/shard_map/dot_general | solution.py:85
  117.7 10.2 slice_negate_fusion.2
  138.8 11.3 fusion.82
  155.9 76.0 %while.30 = (s32[]{:T(128)}, f32[4,1,4,512,128]{4,3,2,1,0:T(8,128)}, f32[4,1,4,512,1]{3,2,4,1,0:T(4,128)S(1)}, f32[4,1,4,512,1]{3,2,4,1,0:T(4,128)S(1)}, s32[4]{...) while((s32[]{:T(128)}, ...), condition=%wide.region_5.6_spmd.clone, body=%wide.region_2.5_spmd.clone.sunk | while | flops 2187328000 | bytes 68764360 | solution.py:131
  231.9 9.1 convolution_convert_fusion.6
  248.2 269.3 %while.31 = (s32[]{:T(128)}, f32[1,4,2048,128]{3,2,1,0:T(8,128)}, f32[1,4,2048,128]{3,2,1,0:T(8,128)}, f32[4,1,4,512,128]{4,3,0,2,1:T(8,128)}, s32[4]{0:T(128)S(...) while((s32[]{:T(128)}, f32[1,4,2048,128]{3,2,1,0:T(8,128)}, ...), condition=%wide.region_9.10_spmd.clone, body=%wide.region_7.9_spmd.clone.sunk | while | flops 5412749824 | bytes 204546864 | solution.py:194
  251.2 10.4 fusion.152
  263.7 12.9 multiply_reduce_fusion.2
  276.6 14.9 multiply_convert_fusion.3
  291.5 8.5 bitcast_add_fusion.4
  303.3 10.6 bitcast_add_fusion.5
  316.4 10.4 fusion.152
  328.9 12.9 multiply_reduce_fusion.2
  341.9 14.9 multiply_convert_fusion.3
  356.7 9.8 bitcast_add_fusion.4
  369.8 11.9 bitcast_add_fusion.5
  384.2 10.4 fusion.152
  396.8 12.9 multiply_reduce_fusion.2
  409.7 14.9 multiply_convert_fusion.3
  424.6 9.8 bitcast_add_fusion.4
  437.6 11.9 bitcast_add_fusion.5
  452.1 10.4 fusion.152
  464.6 12.9 multiply_reduce_fusion.2
  477.6 14.9 multiply_convert_fusion.3
  492.4 9.8 bitcast_add_fusion.4
  505.5 11.9 bitcast_add_fusion.5
  537.7 7.1 pad_add_fusion.1
  554.9 8.7 copy.78
  570.5 21.5 %fusion.100 = f32[2048,2048]{1,0:T(8,128)S(1)} fusion(bf16[2048,2048]{1,0:T(8,128)(2,1)} %all-gather.6.cloned.1.call-done, bf16[2048,2048]{1,0:T(8,128)(2,1)} %param.29), kind=kOutput, calls=%fused_computation.164 | convolution fusion | flops 17179869184 | bytes 33554432 | tf_op jit(solution)/shard_map/dot_general | solution.py:137
  592.0 61.6 %fusion.96 = (bf16[2048]{0:T(1024)(128)(2,1)}, bf16[2048,2048]{1,0:T(8,128)(2,1)}, f32[2048,2048]{1,0:T(8,128)}) fusion(f32[2048,2048]{1,0:T(8,128)S(1)} %fusion.100, f32[2048]{0:T(1024)S(1)} %copy-done.29, bf16[2048,2048]{1,0:T(8,128)(2,1)} %all-gather.8.cloned.1.call-done, bf16[2048,2048]{1,0:T(8,128)(2,1)} %param.31), kind=kOutput, calls=%fused_computation.161 | convolution fusion | flops 17490245632 | bytes 58732544 | tf_op jit(solution)/shard_map/dot_general | solution.py:44
  653.7 11.1 multiply_convert_fusion.1
  664.8 19.8 %convolution_convert_fusion.4 = bf16[2048,1536]{1,0:T(8,128)(2,1)} fusion(bf16[2048,2048]{1,0:T(8,128)(2,1)} %all-gather.4.cloned.1.call-done, bf16[2048,1536]{0,1:T(8,128)(2,1)} %bitcast.188), kind=kOutput, calls=%fused_computation.81 | convolution fusion | flops 12888047616 | bytes 20971520 | tf_op jit(solution)/shard_map/dot_general | solution.py:38
  684.6 20.7 %convolution_convert_fusion = bf16[2048,2048]{1,0:T(8,128)(2,1)} fusion(bf16[2048,2048]{1,0:T(8,128)(2,1)S(1)} %copy-done.17, bf16[2048,2048]{1,0:T(8,128)(2,1)S(1)} %bitcast.187), kind=kOutput, calls=%fused_computation.77 | convolution fusion | flops 17184063488 | bytes 25165824 | tf_op jit(solution)/shard_map/dot_general | solution.py:38
  705.3 22.5 %convolution_convert_fusion.1 = bf16[2048,2048]{1,0:T(8,128)(2,1)} fusion(bf16[2048,2048]{1,0:T(8,128)(2,1)S(1)} %copy-done.44, bf16[2048,2048]{1,0:T(8,128)(2,1)} %get-tuple-element.273), kind=kOutput, calls=%fused_computation.78 | convolution fusion | flops 17184063488 | bytes 25165824 | tf_op jit(solution)/shard_map/dot_general | solution.py:38
  734.0 17.6 convolution_convert_fusion.3
  751.5 22.4 %convolution_convert_fusion.2 = bf16[2048,2048]{1,0:T(8,128)(2,1)S(1)} fusion(bf16[2048,2048]{1,0:T(8,128)(2,1)} %get-tuple-element.273, bf16[2048,2048]{1,0:T(8,128)(2,1)} %param.29), kind=kOutput, calls=%fused_computation.79 | convolution fusion | flops 17184063488 | bytes 25165824 | tf_op jit(solution)/shard_map/dot_general | solution.py:44
  780.6 11.2 fusion.92
  791.8 26.5 %convolution_add_fusion.1 = f32[2048,2048]{1,0:T(8,128)} fusion(f32[2048,2048]{1,0:T(8,128)} %fusion.92, bf16[2048,2048]{1,0:T(8,128)(2,1)} %multiply_convert_fusion.1, bf16[2048,2048]{1,0:T(8,128)(2,1)} %param.31), kind=kOutput, calls=%fused_computation.76 | convolution fusion | flops 17184063488 | bytes 50331648 | tf_op jit(solution)/shard_map/dot_general | solution.py:143
  823.9 39.9 %all-reduce.9 = (bf16[1536]{0:T(1024)(128)(2,1)S(1)}, bf16[2048]{0:T(1024)(128)(2,1)S(1)}, bf16[2048]{0:T(1024)(128)(2,1)S(1)}) all-reduce(bf16[1536]{0:T(1024)(128)(2,1)S(1)} %reduce_sum.171, bf16[2048]{0:T(1024)(128)(2,1)S(1)} %reduce_sum.172, bf16[2048]{0:T(1024)(128)(2,1)S(1)} %copy-done.43), channel_id=1, replica_groups=mesh['dp'=8,'tensor'=4] {'dp'}, use_global_device_ids=true, to_apply=%region_25.26 | all-reduce | flops 5632 | bytes 22528 | tf_op jit(solution)/shard_map/psum | solution.py:222
  864.9 621.0 %all-reduce.13.cloned.1.call-done = (bf16[2048,1536]{1,0:T(8,128)(2,1)}, bf16[512,2048]{1,0:T(8,128)(2,1)}, bf16[2048,2048]{1,0:T(8,128)(2,1)}, bf16[2048,2048]{1,0:T(8,128)(2,1)}) async-done(((bf16[2048,1536]{1,0:T(8,128)(2,1)}, bf16[512,2048]{1,0:T(8,128)(2,1)}, bf16[2048,2048]{1,0:T(8,128)(2,1)}, bf16[2048,2048]{1,0:T(8,128)(2,1)}), (bf16[2048,1536]{1,0:T(8,128)(2,1)}, bf16[512,2048]{1,0:T(8,128)(2,1)}, ...) | async-done | bytes 25165840 | tf_op jit(solution)/shard_map/psum | solution.py:221
  1485.9 14.5 convert_element_type.209
  1500.3 14.6 convert_element_type.212
  1515.0 9.5 convert_element_type.203
  1527.0 86.6 %reduce-scatter.5.cloned.1.call-done = bf16[512,4096]{1,0:T(8,128)(2,1)} async-done(((bf16[2048,4096]{1,0:T(8,128)(2,1)}), bf16[512,4096]{1,0:T(8,128)(2,1)}) %reduce-scatter.5.cloned.1.call-update) | async-done | bytes 4194320 | tf_op jit(solution)/shard_map/reduce_scatter | solution.py:206
  1623.9 40.6 %all-reduce.8 = (f32[2048]{0:T(1024)}, f32[2048]{0:T(1024)}, f32[2048]{0:T(1024)}, f32[2048]{0:T(1024)}) all-reduce(f32[2048]{0:T(1024)S(1)} %get-tuple-element.210, f32[2048]{0:T(1024)S(1)} %get-tuple-element.216, f32[2048]{0:T(1024)S(1)} %get-tuple-element.209, ...), channel_id=1, replica_groups=mesh['dp'=8,'tensor'=4] {'dp','tensor'}, use_global_device_ids=true, to_apply=%region_16.17 | all-reduce | flops 8192 | bytes 65536 | tf_op jit(solution)/shard_map/psum | solution.py:217
  1664.5 78.4 %reduce-scatter.3.cloned.1.call-done = f32[512,2048]{1,0:T(8,128)} async-done(((f32[2048,2048]{1,0:T(8,128)}), f32[512,2048]{1,0:T(8,128)}) %reduce-scatter.3.cloned.1.call-update) | async-done | bytes 4194320 | tf_op jit(solution)/shard_map/reduce_scatter | solution.py:141
  1742.9 9.4 add_add_fusion.2
  (253 shorter events, 225.2 us)
Async XLA Ops:
  7.2 224.8 %copy-start = (bf16[512,2048]{1,0:T(8,128)(2,1)S(1)}, bf16[512,2048]{1,0:T(8,128)(2,1)}, u32[]{:S(2)}) copy-start(bf16[512,2048]{1,0:T(8,128)(2,1)} %param.27) | copy-start | bytes 6291460
  7.2 5.1 copy-start.35
  7.2 5.1 copy-start.36
  7.2 5.1 copy-start.37
  7.2 5.1 copy-start.38
  7.2 69.8 %all-gather.4.cloned.1.call-start = ((), (), s32[]{:S(2)}) async-start(), calls=%async_computation.2 | async-start | bytes 10485760 | tf_op jit(solution)/shard_map/all_gather | solution.py:82
  7.3 5.1 copy-start.8
  9.4 6.5 copy-start.24
  15.9 8.3 copy-start.40
  15.9 216.0 %all-gather.8.cloned.1.call-start = ((), (), s32[]{:S(2)}) async-start(), calls=%async_computation.5 | async-start | bytes 10485760 | tf_op jit(solution)/shard_map/all_gather | solution.py:151
  16.7 553.9 %all-gather.6.cloned.1.call-start = ((), (), s32[]{:S(2)}) async-start(), calls=%async_computation.3 | async-start | bytes 10485760 | tf_op jit(solution)/shard_map/all_gather | solution.py:83
  17.4 1468.5 %all-reduce.13.cloned.1.call-start = ((), (), s32[]{:S(2)}) async-start(), calls=%async_computation.7 | async-start | bytes 50331648 | tf_op jit(solution)/shard_map/psum | solution.py:221
  21.1 117.7 %copy-start.13 = (f32[2048,32]{1,0:T(8,128)}, f32[2048,32]{1,0:T(8,128)S(1)}, u32[]{:S(2)}) copy-start(f32[2048,32]{1,0:T(8,128)S(1)} %copy.71) | copy-start | bytes 786436
  95.1 7.6 copy-start.15
  113.4 4.3 copy-start.7
  138.8 11.3 copy-start.16
  165.0 3.9 copy-start.10
  203.0 3.9 copy-start.10
  222.0 3.9 copy-start.10
  241.0 3.9 copy-start.32
  251.1 12.5 copy-start.3
  291.5 8.5 copy-start.1
  291.5 8.5 copy-start.4
  316.4 12.5 copy-start.3
  356.7 9.8 copy-start.1
  356.7 9.8 copy-start.4
  384.2 12.5 copy-start.3
  424.6 9.8 copy-start.1
  424.6 9.8 copy-start.4
  452.1 12.5 copy-start.3
  492.4 9.8 copy-start.1
  492.4 9.8 copy-start.4
  533.0 4.8 copy-start.14
  570.5 21.5 %copy-start.29 = (f32[2048]{0:T(1024)S(1)}, f32[2048]{0:T(1024)}, u32[]{:S(2)}) copy-start(f32[2048]{0:T(1024)} %convert_element_type.190) | copy-start | bytes 24580
  653.7 30.9 %slice-start = ((s8[8388608]{0:T(1024)(128)(4,1)}), s8[4194304]{0:T(1024)(128)(4,1)S(1)}, s32[]{:S(2)}) async-start(s8[8388608]{0:T(1024)(128)(4,1)} %bitcast.186), calls=%async_computation.8 | async-start | bytes 8388608
  664.8 19.8 %slice-start.1 = ((s8[8388608]{0:T(1024)(128)(4,1)}), s8[4194304]{0:T(1024)(128)(4,1)S(1)}, s32[]{:S(2)}) async-start(s8[8388608]{0:T(1024)(128)(4,1)} %bitcast.186), calls=%async_computation.9 | async-start | bytes 8388608
  664.8 19.8 %copy-start.17 = (bf16[2048,2048]{1,0:T(8,128)(2,1)S(1)}, bf16[2048,2048]{1,0:T(8,128)(2,1)}, u32[]{:S(2)}) copy-start(bf16[2048,2048]{1,0:T(8,128)(2,1)} %multiply_convert_fusion.1) | copy-start | bytes 25165828
  684.6 20.7 %copy-start.44 = (bf16[2048,2048]{1,0:T(8,128)(2,1)S(1)}, bf16[2048,2048]{1,0:T(8,128)(2,1)}, u32[]{:S(2)}) copy-start(bf16[2048,2048]{1,0:T(8,128)(2,1)} %all-gather.6.cloned.1.call-done) | copy-start | bytes 25165828
  705.3 22.5 %copy-start.18 = (f32[1,4,512,4,128]{4,3,2,1,0:T(4,128)S(1)}, f32[1,4,512,4,128]{4,3,2,1,0:T(4,128)}, u32[]{:S(2)}) copy-start(f32[1,4,512,4,128]{4,3,2,1,0:T(4,128)} %copy.75) | copy-start | bytes 12582916
  705.3 22.5 %copy-start.34 = (f32[2048]{0:T(1024)S(1)}, f32[2048]{0:T(1024)}, u32[]{:S(2)}) copy-start(f32[2048]{0:T(1024)} %fusion.88) | copy-start | bytes 24580
  733.9 879.7 %reduce-scatter.5.cloned.1.call-start = ((), (), s32[]{:S(2)}) async-start(), calls=%async_computation.6 | async-start | bytes 20971520 | tf_op jit(solution)/shard_map/reduce_scatter | solution.py:206
  780.6 962.3 %reduce-scatter.3.cloned.1.call-start = ((), (), s32[]{:S(2)}) async-start(), calls=%async_computation.4 | async-start | bytes 20971520 | tf_op jit(solution)/shard_map/reduce_scatter | solution.py:141
  819.1 4.8 copy-start.43
  863.7 888.6 %copy-start.26 = (f32[2048]{0:T(1024)}, f32[2048]{0:T(1024)S(1)}, u32[]{:S(2)}) copy-start(f32[2048]{0:T(1024)S(1)} %convert_element_type.207) | copy-start | bytes 24580
  1515.0 9.5 copy-start.19
  1527.0 90.0 %copy-start.21 = (f32[2048]{0:T(1024)S(1)}, f32[2048]{0:T(1024)}, u32[]{:S(2)}) copy-start(f32[2048]{0:T(1024)} %copy-done.20) | copy-start | bytes 24580
  1527.0 90.0 %copy-start.23 = (f32[2048]{0:T(1024)S(1)}, f32[2048]{0:T(1024)}, u32[]{:S(2)}) copy-start(f32[2048]{0:T(1024)} %copy-done.22) | copy-start | bytes 24580
  1527.0 90.0 %copy-start.25 = (f32[512]{0:T(512)S(1)}, f32[512]{0:T(512)}, u32[]{:S(2)}) copy-start(f32[512]{0:T(512)} %copy-done.24) | copy-start | bytes 6148
  (17 other events, 43.7 us)
Sparse Core Ops, SparseCore 0:
  16.0 60.9 all-gather.3
  78.6 58.2 all-gather.7
  139.1 58.2 all-gather.5
  734.0 751.7 all-reduce.12
  1488.5 125.0 reduce-scatter.4
  1616.0 126.8 reduce-scatter.2
where the time goes:
time: 1760 us
  waiting for transfers between devices  840 us (48%)
  matrix products  489 us (28%)
  other arithmetic  246 us (14%)
  blocking collectives  80.4 us (5%)
  local copies, waits for them, and re-layouts  71.8 us (4%)
    psum x1, waiting for transfers between devices, shards(): lax.psum(qkv_grad.astype(jnp.bfloat16), 'dp').astype(jnp.float32)  621 us
    dot_general x4, matrix products, times_transposed(): lax.dot_general(left, right, (((1,), (1,)), ((), ())), preferred_element_...  111 us
    reduce_scatter x1, waiting for transfers between devices, shards(): lax.psum_scatter(jnp.concatenate([times_transposed(packed_grad, w_qkv), t...  86.6 us
    reduce_scatter x1, waiting for transfers between devices, shards(): lax.psum_scatter(jnp.dot(context, w_dense, preferred_element_type=jnp.flo...  78.4 us
    dot_general x8, matrix products, block_scores(): jnp.einsum('bhqd,bhkd->bhqk', query_block, key_rows, preferred_element_ty...  69.6 us
    dot_general x4, matrix products, contract_rows(): lax.dot_general(left, right, (((0,), (0,)), ((), ())), preferred_element_...  69.1 us
    convert_element_type x4, other arithmetic, backward_block(): score_grad = (attn_probs * (probs_grad - centre)).astype(jnp.bfloat16)  59.4 us
    all_gather x1, waiting for transfers between devices, shards(): lax.all_gather(normed_one.astype(jnp.bfloat16), 'tensor', axis=0, tiled=T...  52.2 us
  transfers between devices with their start and end apart: 6, of which 4 were waited for; matrix products, arithmetic and copies ran while one was open for 35% of the time, Pallas kernels for 0%

commit v1 on v0

--- a/solution.py
+++ b/solution.py
@@ -215,7 +215,7 @@
     input_two, gain_two, bias_two = back_two(normed_grads[:, width:])
     in_grad = out_grad.astype(jnp.float32) + input_one + input_two
     gain_one, bias_one, gain_two, bias_two = lax.psum(
-        (gain_one, bias_one, gain_two, bias_two), ("dp", "tensor")
+        lax.psum((gain_one, bias_one, gain_two, bias_two), "tensor"), "dp"
     )
     qkv_grad, qkv_bias_grad, dense_grad, fc1_grad, fc1_bias_grad, fc2_grad, out_bias_grad = (
         lax.psum(qkv_grad.astype(jnp.bfloat16), "dp").astype(jnp.float32),

time: 1760 us -> 1760 us (level)
    psum x1 -> x2, blocking collectives: 40.6 us -> 48.1 us  [the longest x1 37.8 us: shards(): lax.psum(lax.psum((gain_one, bias_one, gain_two, bias_two), 'tensor'), 'dp')]
where the time goes in v1:
time: 1760 us
  waiting for transfers between devices  831 us (47%)
  matrix products  489 us (28%)
  other arithmetic  246 us (14%)
  blocking collectives  87.9 us (5%)
  local copies, waits for them, and re-layouts  71.8 us (4%)
    psum x1, waiting for transfers between devices, shards(): lax.psum(qkv_grad.astype(jnp.bfloat16), 'dp').astype(jnp.float32)  621 us
    dot_general x4, matrix products, times_transposed(): lax.dot_general(left, right, (((1,), (1,)), ((), ())), preferred_element_...  111 us
    reduce_scatter x1, waiting for transfers between devices, shards(): lax.psum_scatter(jnp.concatenate([times_transposed(packed_grad, w_qkv), t...  86.6 us
    reduce_scatter x1, waiting for transfers between devices, shards(): lax.psum_scatter(jnp.dot(context, w_dense, preferred_element_type=jnp.flo...  70.2 us
    dot_general x8, matrix products, block_scores(): jnp.einsum('bhqd,bhkd->bhqk', query_block, key_rows, preferred_element_ty...  69.6 us
    dot_general x4, matrix products, contract_rows(): lax.dot_general(left, right, (((0,), (0,)), ((), ())), preferred_element_...  69.1 us
    convert_element_type x4, other arithmetic, backward_block(): score_grad = (attn_probs * (probs_grad - centre)).astype(jnp.bfloat16)  59.4 us
    all_gather x1, waiting for transfers between devices, shards(): lax.all_gather(normed_one.astype(jnp.bfloat16), 'tensor', axis=0, tiled=T...  52.2 us
  transfers between devices with their start and end apart: 6, of which 4 were waited for; matrix products, arithmetic and copies ran while one was open for 35% of the time, Pallas kernels for 0%

profile of v1, /device:TPU:0, one launch (start us, length us, event | category | flops | bytes accessed | tf_op | source)
XLA Modules:
  0.0 1759.3 jit_solution(17465997560683955662)
XLA Ops:
  24.8 52.2 %all-gather.4.cloned.1.call-done = bf16[2048,2048]{1,0:T(8,128)(2,1)} async-done(((bf16[512,2048]{1,0:T(8,128)(2,1)}), bf16[2048,2048]{1,0:T(8,128)(2,1)}) %all-gather.4.cloned.1.call-update) | async-done | bytes 8388624 | tf_op jit(solution)/shard_map/all_gather | solution.py:82
  77.0 18.0 %convolution_add_fusion = f32[2048,1536]{0,1:T(8,128)S(1)} fusion(bf16[2048,2048]{1,0:T(8,128)(2,1)} %all-gather.4.cloned.1.call-done, bf16[2048,1536]{1,0:T(8,128)(2,1)} %param.25, f32[1536]{0:T(1024)S(1)} %convert_element_type.182), kind=kOutput, calls=%fused_computation.75 | convolution fusion | flops 12888047616 | bytes 27269120 | tf_op jit(solution)/shard_map/dot_general | solution.py:85
  117.6 10.2 slice_negate_fusion.2
  138.8 11.3 fusion.82
  155.9 76.0 %while.30 = (s32[]{:T(128)}, f32[4,1,4,512,128]{4,3,2,1,0:T(8,128)}, f32[4,1,4,512,1]{3,2,4,1,0:T(4,128)S(1)}, f32[4,1,4,512,1]{3,2,4,1,0:T(4,128)S(1)}, s32[4]{...) while((s32[]{:T(128)}, ...), condition=%wide.region_5.6_spmd.clone, body=%wide.region_2.5_spmd.clone.sunk | while | flops 2187328000 | bytes 68764360 | solution.py:131
  231.9 9.1 convolution_convert_fusion.6
  248.2 269.3 %while.31 = (s32[]{:T(128)}, f32[1,4,2048,128]{3,2,1,0:T(8,128)}, f32[1,4,2048,128]{3,2,1,0:T(8,128)}, f32[4,1,4,512,128]{4,3,0,2,1:T(8,128)}, s32[4]{0:T(128)S(...) while((s32[]{:T(128)}, f32[1,4,2048,128]{3,2,1,0:T(8,128)}, ...), condition=%wide.region_9.10_spmd.clone, body=%wide.region_7.9_spmd.clone.sunk | while | flops 5412749824 | bytes 204546864 | solution.py:194
  251.1 10.4 fusion.152
  263.7 12.9 multiply_reduce_fusion.2
  276.6 14.9 multiply_convert_fusion.3
  291.5 8.5 bitcast_add_fusion.4
  303.3 10.6 bitcast_add_fusion.5
  316.4 10.4 fusion.152
  328.9 12.9 multiply_reduce_fusion.2
  341.9 14.9 multiply_convert_fusion.3
  356.7 9.8 bitcast_add_fusion.4
  369.8 11.9 bitcast_add_fusion.5
  384.2 10.4 fusion.152
  396.8 12.9 multiply_reduce_fusion.2
  409.7 14.9 multiply_convert_fusion.3
  424.6 9.8 bitcast_add_fusion.4
  437.6 11.9 bitcast_add_fusion.5
  452.1 10.4 fusion.152
  464.6 12.9 multiply_reduce_fusion.2
  477.5 14.9 multiply_convert_fusion.3
  492.4 9.8 bitcast_add_fusion.4
  505.5 11.9 bitcast_add_fusion.5
  554.9 8.7 copy.78
  570.5 21.5 %fusion.100 = f32[2048,2048]{1,0:T(8,128)S(1)} fusion(bf16[2048,2048]{1,0:T(8,128)(2,1)} %all-gather.6.cloned.1.call-done, bf16[2048,2048]{1,0:T(8,128)(2,1)} %param.29), kind=kOutput, calls=%fused_computation.164 | convolution fusion | flops 17179869184 | bytes 33554432 | tf_op jit(solution)/shard_map/dot_general | solution.py:137
  592.1 61.6 %fusion.96 = (bf16[2048]{0:T(1024)(128)(2,1)}, bf16[2048,2048]{1,0:T(8,128)(2,1)}, f32[2048,2048]{1,0:T(8,128)}) fusion(f32[2048,2048]{1,0:T(8,128)S(1)} %fusion.100, f32[2048]{0:T(1024)S(1)} %copy-done.29, bf16[2048,2048]{1,0:T(8,128)(2,1)} %all-gather.8.cloned.1.call-done, bf16[2048,2048]{1,0:T(8,128)(2,1)} %param.31), kind=kOutput, calls=%fused_computation.161 | convolution fusion | flops 17490245632 | bytes 58732544 | tf_op jit(solution)/shard_map/dot_general | solution.py:44
  653.7 11.1 multiply_convert_fusion.1
  664.8 19.9 %convolution_convert_fusion.4 = bf16[2048,1536]{1,0:T(8,128)(2,1)} fusion(bf16[2048,2048]{1,0:T(8,128)(2,1)} %all-gather.4.cloned.1.call-done, bf16[2048,1536]{0,1:T(8,128)(2,1)} %bitcast.188), kind=kOutput, calls=%fused_computation.81 | convolution fusion | flops 12888047616 | bytes 20971520 | tf_op jit(solution)/shard_map/dot_general | solution.py:38
  684.7 20.7 %convolution_convert_fusion = bf16[2048,2048]{1,0:T(8,128)(2,1)} fusion(bf16[2048,2048]{1,0:T(8,128)(2,1)S(1)} %copy-done.17, bf16[2048,2048]{1,0:T(8,128)(2,1)S(1)} %bitcast.187), kind=kOutput, calls=%fused_computation.77 | convolution fusion | flops 17184063488 | bytes 25165824 | tf_op jit(solution)/shard_map/dot_general | solution.py:38
  705.4 22.5 %convolution_convert_fusion.1 = bf16[2048,2048]{1,0:T(8,128)(2,1)} fusion(bf16[2048,2048]{1,0:T(8,128)(2,1)S(1)} %copy-done.44, bf16[2048,2048]{1,0:T(8,128)(2,1)} %get-tuple-element.277), kind=kOutput, calls=%fused_computation.78 | convolution fusion | flops 17184063488 | bytes 25165824 | tf_op jit(solution)/shard_map/dot_general | solution.py:38
  734.0 17.6 convolution_convert_fusion.3
  751.6 22.4 %convolution_convert_fusion.2 = bf16[2048,2048]{1,0:T(8,128)(2,1)S(1)} fusion(bf16[2048,2048]{1,0:T(8,128)(2,1)} %get-tuple-element.277, bf16[2048,2048]{1,0:T(8,128)(2,1)} %param.29), kind=kOutput, calls=%fused_computation.79 | convolution fusion | flops 17184063488 | bytes 25165824 | tf_op jit(solution)/shard_map/dot_general | solution.py:44
  780.7 11.2 fusion.92
  791.9 26.6 %convolution_add_fusion.1 = f32[2048,2048]{1,0:T(8,128)} fusion(f32[2048,2048]{1,0:T(8,128)} %fusion.92, bf16[2048,2048]{1,0:T(8,128)(2,1)} %multiply_convert_fusion.1, bf16[2048,2048]{1,0:T(8,128)(2,1)} %param.31), kind=kOutput, calls=%fused_computation.76 | convolution fusion | flops 17184063488 | bytes 50331648 | tf_op jit(solution)/shard_map/dot_general | solution.py:143
  824.0 39.8 %all-reduce.10 = (bf16[1536]{0:T(1024)(128)(2,1)S(1)}, bf16[2048]{0:T(1024)(128)(2,1)S(1)}, bf16[2048]{0:T(1024)(128)(2,1)S(1)}) all-reduce(bf16[1536]{0:T(1024)(128)(2,1)S(1)} %reduce_sum.171, bf16[2048]{0:T(1024)(128)(2,1)S(1)} %reduce_sum.172, bf16[2048]{0:T(1024)(128)(2,1)S(1)} %copy-done.43), channel_id=1, replica_groups=mesh['dp'=8,'tensor'=4] {'dp'}, use_global_device_ids=true, to_apply=%region_29.30 | all-reduce | flops 5632 | bytes 22528 | tf_op jit(solution)/shard_map/psum | solution.py:222
  865.0 620.9 %all-reduce.14.cloned.1.call-done = (bf16[2048,1536]{1,0:T(8,128)(2,1)}, bf16[512,2048]{1,0:T(8,128)(2,1)}, bf16[2048,2048]{1,0:T(8,128)(2,1)}, bf16[2048,2048]{1,0:T(8,128)(2,1)}) async-done(((bf16[2048,1536]{1,0:T(8,128)(2,1)}, bf16[512,2048]{1,0:T(8,128)(2,1)}, bf16[2048,2048]{1,0:T(8,128)(2,1)}, bf16[2048,2048]{1,0:T(8,128)(2,1)}), (bf16[2048,1536]{1,0:T(8,128)(2,1)}, bf16[512,2048]{1,0:T(8,128)(2,1)}, ...) | async-done | bytes 25165840 | tf_op jit(solution)/shard_map/psum | solution.py:221
  1485.9 14.5 convert_element_type.209
  1500.4 14.6 convert_element_type.212
  1515.0 9.5 convert_element_type.203
  1527.1 86.6 %reduce-scatter.5.cloned.1.call-done = bf16[512,4096]{1,0:T(8,128)(2,1)} async-done(((bf16[2048,4096]{1,0:T(8,128)(2,1)}), bf16[512,4096]{1,0:T(8,128)(2,1)}) %reduce-scatter.5.cloned.1.call-update) | async-done | bytes 4194320 | tf_op jit(solution)/shard_map/reduce_scatter | solution.py:206
  1623.9 10.3 all-reduce.9
  1634.2 37.8 %all-reduce.8 = (f32[2048]{0:T(1024)}, f32[2048]{0:T(1024)}, f32[2048]{0:T(1024)}, f32[2048]{0:T(1024)}) all-reduce(f32[2048]{0:T(1024)S(1)} %get-tuple-element.265, f32[2048]{0:T(1024)S(1)} %get-tuple-element.266, f32[2048]{0:T(1024)S(1)} %get-tuple-element.267, ...), channel_id=1, replica_groups=mesh['dp'=8,'tensor'=4] {'dp'}, use_global_device_ids=true, to_apply=%region_17.18 | all-reduce | flops 8192 | bytes 65536 | tf_op jit(solution)/shard_map/psum | solution.py:217
  1672.0 70.2 %reduce-scatter.3.cloned.1.call-done = f32[512,2048]{1,0:T(8,128)} async-done(((f32[2048,2048]{1,0:T(8,128)}), f32[512,2048]{1,0:T(8,128)}) %reduce-scatter.3.cloned.1.call-update) | async-done | bytes 4194320 | tf_op jit(solution)/shard_map/reduce_scatter | solution.py:141
  1742.3 9.4 add_add_fusion.2
  (254 shorter events, 232.3 us)
Async XLA Ops:
  7.2 224.8 %copy-start = (bf16[512,2048]{1,0:T(8,128)(2,1)S(1)}, bf16[512,2048]{1,0:T(8,128)(2,1)}, u32[]{:S(2)}) copy-start(bf16[512,2048]{1,0:T(8,128)(2,1)} %param.27) | copy-start | bytes 6291460
  7.2 5.1 copy-start.35
  7.2 5.1 copy-start.36
  7.2 5.1 copy-start.37
  7.2 5.1 copy-start.38
  7.2 69.8 %all-gather.4.cloned.1.call-start = ((), (), s32[]{:S(2)}) async-start(), calls=%async_computation.2 | async-start | bytes 10485760 | tf_op jit(solution)/shard_map/all_gather | solution.py:82
  7.3 5.1 copy-start.8
  9.4 6.4 copy-start.24
  15.9 8.3 copy-start.40
  15.9 216.0 %all-gather.8.cloned.1.call-start = ((), (), s32[]{:S(2)}) async-start(), calls=%async_computation.5 | async-start | bytes 10485760 | tf_op jit(solution)/shard_map/all_gather | solution.py:151
  16.7 553.9 %all-gather.6.cloned.1.call-start = ((), (), s32[]{:S(2)}) async-start(), calls=%async_computation.3 | async-start | bytes 10485760 | tf_op jit(solution)/shard_map/all_gather | solution.py:83
  17.4 1468.6 %all-reduce.14.cloned.1.call-start = ((), (), s32[]{:S(2)}) async-start(), calls=%async_computation.7 | async-start | bytes 50331648 | tf_op jit(solution)/shard_map/psum | solution.py:221
  21.1 117.7 %copy-start.13 = (f32[2048,32]{1,0:T(8,128)}, f32[2048,32]{1,0:T(8,128)S(1)}, u32[]{:S(2)}) copy-start(f32[2048,32]{1,0:T(8,128)S(1)} %copy.71) | copy-start | bytes 786436
  95.1 7.6 copy-start.15
  113.3 4.3 copy-start.7
  138.8 11.3 copy-start.16
  165.0 3.9 copy-start.10
  184.0 3.9 copy-start.10
  203.0 3.9 copy-start.10
  241.0 3.9 copy-start.32
  251.1 12.5 copy-start.3
  291.5 8.5 copy-start.1
  291.5 8.5 copy-start.4
  316.4 12.5 copy-start.3
  356.7 9.8 copy-start.1
  356.7 9.8 copy-start.4
  384.2 12.5 copy-start.3
  424.6 9.8 copy-start.1
  424.6 9.8 copy-start.4
  452.1 12.5 copy-start.3
  492.4 9.8 copy-start.1
  492.4 9.8 copy-start.4
  533.0 4.8 copy-start.14
  570.5 21.5 %copy-start.29 = (f32[2048]{0:T(1024)S(1)}, f32[2048]{0:T(1024)}, u32[]{:S(2)}) copy-start(f32[2048]{0:T(1024)} %convert_element_type.190) | copy-start | bytes 24580
  653.7 31.0 %slice-start = ((s8[8388608]{0:T(1024)(128)(4,1)}), s8[4194304]{0:T(1024)(128)(4,1)S(1)}, s32[]{:S(2)}) async-start(s8[8388608]{0:T(1024)(128)(4,1)} %bitcast.186), calls=%async_computation.8 | async-start | bytes 8388608
  664.8 19.9 %slice-start.1 = ((s8[8388608]{0:T(1024)(128)(4,1)}), s8[4194304]{0:T(1024)(128)(4,1)S(1)}, s32[]{:S(2)}) async-start(s8[8388608]{0:T(1024)(128)(4,1)} %bitcast.186), calls=%async_computation.9 | async-start | bytes 8388608
  664.8 19.9 %copy-start.17 = (bf16[2048,2048]{1,0:T(8,128)(2,1)S(1)}, bf16[2048,2048]{1,0:T(8,128)(2,1)}, u32[]{:S(2)}) copy-start(bf16[2048,2048]{1,0:T(8,128)(2,1)} %multiply_convert_fusion.1) | copy-start | bytes 25165828
  684.7 20.7 %copy-start.44 = (bf16[2048,2048]{1,0:T(8,128)(2,1)S(1)}, bf16[2048,2048]{1,0:T(8,128)(2,1)}, u32[]{:S(2)}) copy-start(bf16[2048,2048]{1,0:T(8,128)(2,1)} %all-gather.6.cloned.1.call-done) | copy-start | bytes 25165828
  705.4 22.5 %copy-start.18 = (f32[1,4,512,4,128]{4,3,2,1,0:T(4,128)S(1)}, f32[1,4,512,4,128]{4,3,2,1,0:T(4,128)}, u32[]{:S(2)}) copy-start(f32[1,4,512,4,128]{4,3,2,1,0:T(4,128)} %copy.75) | copy-start | bytes 12582916
  705.4 22.5 %copy-start.34 = (f32[2048]{0:T(1024)S(1)}, f32[2048]{0:T(1024)}, u32[]{:S(2)}) copy-start(f32[2048]{0:T(1024)} %fusion.88) | copy-start | bytes 24580
  734.0 879.7 %reduce-scatter.5.cloned.1.call-start = ((), (), s32[]{:S(2)}) async-start(), calls=%async_computation.6 | async-start | bytes 20971520 | tf_op jit(solution)/shard_map/reduce_scatter | solution.py:206
  780.7 961.6 %reduce-scatter.3.cloned.1.call-start = ((), (), s32[]{:S(2)}) async-start(), calls=%async_computation.4 | async-start | bytes 20971520 | tf_op jit(solution)/shard_map/reduce_scatter | solution.py:141
  819.2 4.8 copy-start.43
  863.8 887.8 %copy-start.26 = (f32[2048]{0:T(1024)}, f32[2048]{0:T(1024)S(1)}, u32[]{:S(2)}) copy-start(f32[2048]{0:T(1024)S(1)} %convert_element_type.207) | copy-start | bytes 24580
  1515.0 9.5 copy-start.19
  1527.1 90.0 %copy-start.21 = (f32[2048]{0:T(1024)S(1)}, f32[2048]{0:T(1024)}, u32[]{:S(2)}) copy-start(f32[2048]{0:T(1024)} %copy-done.20) | copy-start | bytes 24580
  1527.1 90.0 %copy-start.23 = (f32[2048]{0:T(1024)S(1)}, f32[2048]{0:T(1024)}, u32[]{:S(2)}) copy-start(f32[2048]{0:T(1024)} %copy-done.22) | copy-start | bytes 24580
  1527.1 90.0 %copy-start.25 = (f32[512]{0:T(512)S(1)}, f32[512]{0:T(512)}, u32[]{:S(2)}) copy-start(f32[512]{0:T(512)} %copy-done.24) | copy-start | bytes 6148
  (17 other events, 43.7 us)
Sparse Core Ops, SparseCore 0:
  16.0 60.9 all-gather.3
  78.6 58.2 all-gather.7
  139.0 58.2 all-gather.5
  734.1 751.7 all-reduce.13
  1488.5 125.0 reduce-scatter.4
  1616.1 126.1 reduce-scatter.2
